TPU v7x, 128 devices: a whole 4x4x4 slice. The times are simulated.
128 devices in a mesh: date: 8 (over y, core), strip: 16 (over z, x).
Axes of the slice: x: 4, y: 4, z: 4, core: 2. Of those that a mesh axis runs over, the one named last changes fastest.
Arguments:
- stack: float32 [64, 1024, 2048], P('date', 'strip'), may hold values from -6 to 6
- spatial_taps: float32 [13], replicated, may hold values from 0.2 to 1
- temporal_taps: float32 [2, 5], replicated, may hold values from -0.25 to 0.25
- foot_tile: int32 [16384], P(('date', 'strip')), may hold values from 0 to 1
- foot_row: int32 [16384], P(('date', 'strip')), may hold values from 0 to 63
- foot_count: int32 [16384], P(('date', 'strip')), may hold values from 1 to 128
- foot_owner: int32 [16384, 1], P(('date', 'strip')), may hold values from 0 to 127; in each aligned block of 128 rows (0 to 127, 128 to 255, ...) at most 2 rows name the same one
Outputs:
- residual: float32 [64, 1024, 2048], P(None, 'strip', 'date')
- anomaly: float32 [128, 256, 64], P(('date', 'strip'))
- asset_series: float32 [128, 64], P(('date', 'strip'))
Inputs may be any that keep to these rules, and one draw needn't show every extreme that they name: `foot_owner`: among the footprints of one block, no owner appears more than 2 times, a bound that some block reaches; every owner has some footprint.
All inputs are finite; a program needn't handle non-finite values.
Results may differ from a plain program's by a relative error of at most 0.000075.
Values sent between devices are 32-bit elements; how exact they have to be, the bound alone decides.
A program may use at most 128 MiB of HBM per device.

v0:
```python
import jax
import jax.numpy as jnp
from jax import lax
from jax.sharding import PartitionSpec as P

TILE = 128
RADIUS = 6
REACH = 2
DILATION = 8
PAIR_CAP = 2


def with_halo(value, sides, width):
    for axis, dim in sides:
        peers, length = (lax.axis_size(axis), value.shape[dim])
        up = [(i, (i + 1) % peers) for i in range(peers - 1)]
        down = [(j, i) for i, j in up]
        last = lax.slice_in_dim(value, length - width, length, axis=dim)
        initial = lax.slice_in_dim(value, 0, width, axis=dim)
        before = lax.ppermute(last, axis, up)
        after = lax.ppermute(initial, axis, down)
        value = jnp.concatenate([before, value, after], axis=dim)
    return value


def taps_pass(padded, weights, axis_num, length):
    summed = weights[0] * lax.slice_in_dim(padded, 0, length, axis=axis_num)
    for k in range(1, weights.shape[0]):
        summed = summed + weights[k] * lax.slice_in_dim(padded, k, k + length, axis=axis_num)
    return summed


def temporal_filter(series, temporal_taps):
    date_count = series.shape[0]
    for level_idx, spacing in enumerate((1, DILATION)):
        margin = REACH * spacing
        padded = jnp.pad(series, ((margin, margin), (0, 0), (0, 0)))
        smooth_part = temporal_taps[level_idx, 0] * lax.slice_in_dim(padded, 0, date_count, axis=0)
        for k in range(1, 2 * REACH + 1):
            smooth_part = smooth_part + temporal_taps[level_idx, k] * lax.slice_in_dim(
                padded, k * spacing, k * spacing + date_count, axis=0
            )
        series = series - smooth_part
    return series


def shards(stack, spatial_taps, temporal_taps, foot_tile, foot_row, foot_count, foot_owner):
    weights = spatial_taps / jnp.sum(spatial_taps)
    padded = jnp.pad(stack, ((0, 0), (0, 0), (RADIUS, RADIUS)))
    across = taps_pass(padded, weights, 2, stack.shape[2])
    rimmed = with_halo(across, (("strip", 1),), RADIUS)
    corrected = stack - taps_pass(rimmed, weights, 1, stack.shape[1])
    residual = temporal_filter(
        lax.all_to_all(corrected, "date", split_axis=2, concat_axis=0, tiled=True), temporal_taps
    )
    date_count, row_count, col_count = residual.shape
    tile_view = residual.reshape(date_count, row_count, col_count // TILE, TILE)
    picked = tile_view[:, foot_row, foot_tile, :]
    counts = foot_count.astype(jnp.float32)
    inside = (jnp.arange(TILE, dtype=jnp.int32)[None, :] < foot_count[:, None]).astype(jnp.float32)
    foot_mean = jnp.sum(picked * inside[None], axis=2) / counts[None, :]
    owners = foot_owner[:, 0]
    position = jnp.arange(owners.shape[0], dtype=jnp.int32)
    earlier = (owners[:, None] == owners[None, :]) & (position[None, :] < position[:, None])
    slot_rank = jnp.sum(earlier.astype(jnp.int32), axis=1)
    date_devices = lax.axis_size("date")
    strip_devices = lax.axis_size("strip")
    devices_all = date_devices * strip_devices
    dest_slot = owners * PAIR_CAP + slot_rank
    onehot = (
        dest_slot[:, None] == jnp.arange(devices_all * PAIR_CAP, dtype=jnp.int32)[None, :]
    ).astype(jnp.float32)
    outgoing = jnp.einsum("fk,tf->kt", onehot, foot_mean, precision=lax.Precision.HIGHEST)
    out_weight = jnp.einsum("fk,f->k", onehot, counts, precision=lax.Precision.HIGHEST)
    received, weight_in = (
        lax.all_to_all(
            outgoing.reshape(devices_all, PAIR_CAP, date_count),
            ("date", "strip"),
            split_axis=0,
            concat_axis=0,
            tiled=True,
        ),
        lax.all_to_all(
            out_weight.reshape(devices_all, PAIR_CAP),
            ("date", "strip"),
            split_axis=0,
            concat_axis=0,
            tiled=True,
        ),
    )
    total_weight = jnp.sum(weight_in)
    asset_mean = jnp.sum(weight_in[:, :, None] * received, axis=(0, 1)) / total_weight
    anomaly = jnp.where(weight_in[:, :, None] > 0, received - asset_mean[None, None, :], 0.0)
    return (residual, anomaly.reshape(1, devices_all * PAIR_CAP, date_count), asset_mean[None, :])


def solution(mesh):
    placed = (
        P("date", "strip", None),
        P(),
        P(),
        P(("date", "strip")),
        P(("date", "strip")),
        P(("date", "strip")),
        P(("date", "strip"), None),
    )
    return jax.shard_map(
        shards,
        mesh=mesh,
        in_specs=placed,
        out_specs=(
            P(None, "strip", "date"),
            P(("date", "strip"), None, None),
            P(("date", "strip"), None),
        ),
        check_vma=False,
    )
```

profile of v0, /device:TPU:1, one launch (start us, length us, event | category | flops | bytes accessed | tf_op | source)
XLA Modules:
  0.0 279.2 jit_solution(2231093077993058063)
XLA Ops:
  0.6 1.3 reduce_sum.47
  1.9 1.3 broadcast_divide_fusion.1
  3.9 6.6 %copy.37 = f32[8,64,2048]{2,0,1:T(8,128)} copy(f32[8,64,2048]{2,1,0:T(8,128)} %param.7) | data formatting | bytes 8388608 | tf_op args[0]
  10.5 42.0 %multiply_add_fusion = f32[8,64,2048]{2,0,1:T(8,128)} fusion(f32[8,64,2048]{2,0,1:T(8,128)} %copy.37, f32[]{:T(128)} %bitcast.12, f32[]{:T(128)} %bitcast.11, f32[]{:T(128)} %bitcast.10, f32[]{:T(128)} %bitcast.9, f32[]{:T(128)} %bitcast.8, f32[]{:T(128)} %bitcast.7, f32[]{:T(128)} %bitcast.6, f32[]{:T(128)} %bitcast.5, f32[]{:T(128)} %bitcast.4, ...), kind=kLoop, calls=%fused_computation.79 | loop fusion | flops 26214400 | bytes 8388660 | tf_op jit(solution)/shard_map/add | solution.py:29
  52.6 1.2 fusion.73
  53.7 4.0 %collective-permute-start = (f32[8,6,2048]{2,0,1:T(8,128)S(1)}, f32[8,6,2048]{2,0,1:T(8,128)S(1)}, u32[]{:S(2)}, u32[]{:S(2)}) collective-permute-start(f32[8,6,2048]{2,0,1:T(8,128)S(1)} %get-tuple-element.18), channel_id=1, source_target_pairs={{0,1},{1,2},{2,3},{3,4},{4,5},{5,6},{6,7},{7,8},{8,9},{9,10},{10,1... | collective-permute-start | bytes 1179656 | tf_op jit(solution)/shard_map/ppermute | solution.py:20
  57.7 1.5 collective-permute-start.1
  59.2 6.3 %collective-permute-done = f32[8,6,2048]{2,0,1:T(8,128)S(1)} collective-permute-done((f32[8,6,2048]{2,0,1:T(8,128)S(1)}, f32[8,6,2048]{2,0,1:T(8,128)S(1)}, u32[]{:S(2)}, u32[]{:S(2)}) %collective-permute-start) | collective-permute-done | bytes 393248 | tf_op jit(solution)/shard_map/ppermute | solution.py:20
  65.5 3.8 %collective-permute-done.1 = f32[8,6,2048]{2,0,1:T(8,128)S(1)} collective-permute-done((f32[8,6,2048]{2,0,1:T(8,128)S(1)}, f32[8,6,2048]{2,0,1:T(8,128)S(1)}, u32[]{:S(2)}, u32[]{:S(2)}) %collective-permute-start.1) | collective-permute-done | bytes 393248 | tf_op jit(solution)/shard_map/ppermute | solution.py:21
  69.3 32.9 %fusion.4 = f32[8,64,2048]{2,0,1:T(8,128)} fusion(f32[8,64,2048]{2,0,1:T(8,128)} %multiply_add_fusion, f32[8,6,2048]{2,0,1:T(8,128)S(1)} %collective-permute-done.1, f32[8,6,2048]{2,0,1:T(8,128)S(1)} %collective-permute-done, f32[]{:T(128)} %bitcast.12, f32[]{:T(128)} %bitcast.11, f32[]{:T(128)} %bitcast.10, f32[]{:T(128)} %bitcast.9, f32[]{:T(128)} %bitcast.8, ...), kind=kLoop, calls=%fused_computation.29 | loop fusion | flops 39845888 | bytes 13369396 | tf_op jit(solution)/shard_map/sub | solution.py:52
  102.1 7.5 %copy.38 = f32[8,64,2048]{1,0,2:T(8,128)} copy(f32[8,64,2048]{2,0,1:T(8,128)} %fusion.4) | data formatting | bytes 8388608 | tf_op jit(solution)/shard_map/sub | solution.py:52
  109.6 9.8 %reshape.84 = f32[8,1,131072]{2,1,0:T(1,128)} reshape(f32[2048,8,64]{2,1,0:T(8,128)} %bitcast.46) | data formatting | bytes 8388608
  119.5 6.5 %all-to-all-start = ((f32[8,1,131072]{2,1,0:T(1,128)}), f32[8,1,131072]{2,1,0:T(1,128)}, u32[]{:S(2)}, u32[]{:S(2)}) async-start(f32[8,1,131072]{2,1,0:T(1,128)} %reshape.84), calls=%async_computation | async-start | bytes 8388608 | tf_op jit(solution)/shard_map/all_to_all | solution.py:54
  126.3 0.8 all_to_all.28
  127.9 46.9 %all-to-all-done = f32[8,1,131072]{2,1,0:T(1,128)} async-done(((f32[8,1,131072]{2,1,0:T(1,128)}), f32[8,1,131072]{2,1,0:T(1,128)}, u32[]{:S(2)}, u32[]{:S(2)}) %all-to-all-start) | async-done | bytes 4194336 | tf_op jit(solution)/shard_map/all_to_all | solution.py:54
  174.8 10.6 %all-to-all-start.1 = ((f32[128,1,2]{2,1,0:T(1,128)}), f32[128,1,2]{2,1,0:T(1,128)S(1)}, u32[]{:S(2)}, u32[]{:S(2)}) async-start(f32[128,1,2]{2,1,0:T(1,128)} %bitcast.31), calls=%async_computation.1 | async-start | bytes 131072 | tf_op jit(solution)/shard_map/all_to_all | solution.py:83
  185.9 13.8 %reduce.3 = f32[8,131072]{1,0:T(8,128)} reduce(f32[8,1,131072]{2,1,0:T(1,128)} %all-to-all-done, f32[]{:T(128)} %broadcast.84), dimensions={1}, to_apply=%all_to_all.24.reduce_sub_computation | reduce | bytes 8388612 | tf_op jit(solution)/shard_map/all_to_all | solution.py:54
  199.7 8.7 %reshape.85 = f32[2048,8,64]{2,1,0:T(8,128)} reshape(f32[8,131072]{1,0:T(8,128)} %reduce.3) | data formatting | bytes 8388608
  208.4 6.8 %copy.39 = f32[8,8,64,256]{3,2,1,0:T(8,128)} copy(f32[8,8,64,256]{2,1,3,0:T(8,128)} %bitcast.47) | data formatting | bytes 8388608 | tf_op jit(solution)/shard_map/all_to_all | solution.py:54
  215.1 12.2 %add_subtract_fusion = f32[64,64,256]{2,1,0:T(8,128)S(1)} fusion(f32[64,64,256]{2,1,0:T(8,128)} %bitcast.48, f32[]{:T(128)} %bitcast.20, f32[]{:T(128)} %bitcast.19, f32[]{:T(128)} %bitcast.18, f32[]{:T(128)} %bitcast.17, f32[]{:T(128)} %bitcast.16), kind=kLoop, calls=%fused_computation.72 | loop fusion | flops 10485760 | bytes 8388628 | tf_op jit(solution)/shard_map/sub | solution.py:43
  227.3 6.6 %fusion.38 = f32[64,64,256]{2,1,0:T(8,128)} fusion(f32[64,64,256]{2,1,0:T(8,128)S(1)} %add_subtract_fusion, f32[]{:T(128)} %bitcast.25, f32[]{:T(128)} %bitcast.24, f32[]{:T(128)} %bitcast.23, f32[]{:T(128)} %bitcast.22, f32[]{:T(128)} %bitcast.21), kind=kLoop, calls=%fused_computation.63 | loop fusion | flops 10485760 | bytes 8388628 | tf_op jit(solution)/shard_map/sub | solution.py:43
  233.9 5.8 %reshape.61 = f32[64,64,2,128]{3,2,1,0:T(2,128)} reshape(f32[64,64,256]{2,1,0:T(8,128)} %fusion.38) | data formatting | bytes 8388608 | tf_op jit(solution)/shard_map/reshape | solution.py:57
  239.7 6.5 %copy.41 = f32[64,64,2,128]{3,0,2,1:T(8,128)} copy(f32[64,64,2,128]{3,2,1,0:T(2,128)} %reshape.61) | data formatting | bytes 8388608 | tf_op jit(solution)/shard_map/reshape | solution.py:57
  246.2 5.0 %gather_fusion = f32[128,64,128]{2,1,0:T(8,128)} fusion(f32[64,64,2,128]{3,0,2,1:T(8,128)} %copy.41, s32[128]{0:T(128)S(1)} %fusion.67), kind=kCustom, calls=%fused_computation | custom fusion | bytes 8389632 | tf_op jit(solution)/shard_map/gather | solution.py:58
  251.3 3.4 %multiply_reduce_fusion = f32[128,64]{1,0:T(8,128)S(1)} fusion(f32[128,64,128]{2,1,0:T(8,128)} %gather_fusion, f32[128,128]{1,0:T(8,128)S(1)} %fusion.63), kind=kLoop, calls=%fused_computation.71 | loop fusion | flops 2088960 | bytes 4292608 | tf_op jit(solution)/shard_map/reduce_sum | solution.py:61
  255.0 0.8 reshape.86
  255.8 9.8 %all-to-all-start.2 = ((f32[128,1,128]{2,1,0:T(1,128)}), f32[128,1,128]{2,1,0:T(1,128)S(1)}, u32[]{:S(2)}, u32[]{:S(2)}) async-start(f32[128,1,128]{2,1,0:T(1,128)} %reshape.86), calls=%async_computation.2 | async-start | bytes 131072 | tf_op jit(solution)/shard_map/all_to_all | solution.py:76
  265.6 0.8 reduce_sum.52
  266.4 8.9 %all-to-all-done.2 = f32[128,1,128]{2,1,0:T(1,128)S(1)} async-done(((f32[128,1,128]{2,1,0:T(1,128)}), f32[128,1,128]{2,1,0:T(1,128)S(1)}, u32[]{:S(2)}, u32[]{:S(2)}) %all-to-all-start.2) | async-done | bytes 65568 | tf_op jit(solution)/shard_map/all_to_all | solution.py:76
  275.2 0.8 reduce.4
  277.1 1.2 fusion.76
  278.5 0.7 copy.43
  (26 shorter events, 4.0 us)
Async XLA Ops:
  53.7 11.7 %collective-permute-start = (f32[8,6,2048]{2,0,1:T(8,128)S(1)}, f32[8,6,2048]{2,0,1:T(8,128)S(1)}, u32[]{:S(2)}, u32[]{:S(2)}) collective-permute-start(f32[8,6,2048]{2,0,1:T(8,128)S(1)} %get-tuple-element.18), channel_id=1, source_target_pairs={{0,1},{1,2},{2,3},{3,4},{4,5},{5,6},{6,7},{7,8},{8,9},{9,10},{10,1... | collective-permute-start | bytes 1179656 | tf_op jit(solution)/shard_map/ppermute | solution.py:20
  57.7 11.6 %collective-permute-start.1 = (f32[8,6,2048]{2,0,1:T(8,128)S(1)}, f32[8,6,2048]{2,0,1:T(8,128)S(1)}, u32[]{:S(2)}, u32[]{:S(2)}) collective-permute-start(f32[8,6,2048]{2,0,1:T(8,128)S(1)} %get-tuple-element.19), channel_id=1, source_target_pairs={{1,0},{2,1},{3,2},{4,3},{5,4},{6,5},{7,6},{8,7},{9,8},{10,9},{11,1... | collective-permute-start | bytes 1179656 | tf_op jit(solution)/shard_map/ppermute | solution.py:21
  119.4 6.5 %copy-start.1 = (s32[128]{0:T(128)S(1)}, s32[128]{0:T(128)}, u32[]{:S(2)}) copy-start(s32[128]{0:T(128)} %param.12) | copy-start | bytes 1540
  119.4 6.5 %copy-start.2 = (s32[128,1]{0,1:T(1,128)S(1)}, s32[128,1]{0,1:T(1,128)}, u32[]{:S(2)}) copy-start(s32[128,1]{0,1:T(1,128)} %param.13) | copy-start | bytes 1540
  119.4 7.7 %copy-start = (f32[2,5]{1,0:T(2,128)S(1)}, f32[2,5]{1,0:T(2,128)}, u32[]{:S(2)}) copy-start(f32[2,5]{1,0:T(2,128)} %param.9) | copy-start | bytes 124
  119.4 8.4 %copy-start.3 = (s32[128]{0:T(128)S(1)}, s32[128]{0:T(128)}, u32[]{:S(2)}) copy-start(s32[128]{0:T(128)} %param.11) | copy-start | bytes 1540
  119.4 8.4 %copy-start.4 = (s32[128]{0:T(128)S(1)}, s32[128]{0:T(128)}, u32[]{:S(2)}) copy-start(s32[128]{0:T(128)} %param.10) | copy-start | bytes 1540
  119.5 55.4 %all-to-all-start = ((f32[8,1,131072]{2,1,0:T(1,128)}), f32[8,1,131072]{2,1,0:T(1,128)}, u32[]{:S(2)}, u32[]{:S(2)}) async-start(f32[8,1,131072]{2,1,0:T(1,128)} %reshape.84), calls=%async_computation | async-start | bytes 8388608 | tf_op jit(solution)/shard_map/all_to_all | solution.py:54
  174.8 80.9 %all-to-all-start.1 = ((f32[128,1,2]{2,1,0:T(1,128)}), f32[128,1,2]{2,1,0:T(1,128)S(1)}, u32[]{:S(2)}, u32[]{:S(2)}) async-start(f32[128,1,2]{2,1,0:T(1,128)} %bitcast.31), calls=%async_computation.1 | async-start | bytes 131072 | tf_op jit(solution)/shard_map/all_to_all | solution.py:83
  255.8 19.5 %all-to-all-start.2 = ((f32[128,1,128]{2,1,0:T(1,128)}), f32[128,1,128]{2,1,0:T(1,128)S(1)}, u32[]{:S(2)}, u32[]{:S(2)}) async-start(f32[128,1,128]{2,1,0:T(1,128)} %reshape.86), calls=%async_computation.2 | async-start | bytes 131072 | tf_op jit(solution)/shard_map/all_to_all | solution.py:76
where the time goes:
time: 281 us; the launch traced here: 279 us
  other arithmetic  118 us (42%)
  waiting for transfers between devices  65.9 us (23%)
  local copies, waits for them, and re-layouts  62.2 us (22%)
  starting transfers between devices  32.2 us (11%)
    all_to_all x1, waiting for transfers between devices, shards(): lax.all_to_all(corrected, 'date', split_axis=2, concat_axis=0, tiled=True)  46.9 us
    add x1, other arithmetic, taps_pass(): summed + weights[k] * lax.slice_in_dim(padded, k, k + length, axis=axis_num)  42 us
    sub x1, other arithmetic, shards(): corrected = stack - taps_pass(rimmed, weights, 1, stack.shape[1])  32.9 us
    unnamed x16, local copies, waits for them, and re-layouts  26.8 us
    sub x2, other arithmetic, temporal_filter(): series = series - smooth_part  18.8 us
    all_to_all x1, other arithmetic, shards(): lax.all_to_all(corrected, 'date', split_axis=2, concat_axis=0, tiled=True)  13.8 us
    reshape x2, local copies, waits for them, and re-layouts, shards(): tile_view = residual.reshape(date_count, row_count, col_count // TILE, TILE)  12.3 us
    all_to_all x1, starting transfers between devices, shards(): lax.all_to_all(out_weight.reshape(devices_all, PAIR_CAP), ('date', 'strip...  10.6 us
  transfers between devices with their start and end apart: 5, of which 4 were waited for; matrix products, arithmetic and copies ran while one was open for 26% of the time, Pallas kernels for 0%

commit v1 on v0

v1 whole, which is shorter than its diff:
```python
import functools
import jax
import jax.numpy as jnp
from jax import lax
from jax.experimental import pallas as pl
from jax.experimental.pallas import tpu as pltpu
from jax.sharding import PartitionSpec as P

MESH = pl.DeviceIdType.MESH
F32, BF16, I32 = jnp.float32, jnp.bfloat16, jnp.int32
ND, NS = 8, 16
T, TL = 64, 8
R, G = 64, 8
C, CB = 2048, 256
F = 128
RAD = 6
HELD = 2


def dot(a, b):
    return jnp.dot(a, b, preferred_element_type=F32)


def split(x):
    hi = x.astype(BF16)
    return hi, (x - hi.astype(F32)).astype(BF16)


def iota(shape, dim):
    return lax.broadcasted_iota(I32, shape, dim)


def kernel(
    stack, spat, temp, ftile, frow, fcount, fowner,
    res_out, anom_out, asset_out,
    win, rp, b0h, b0l, b1h, b1l, sbuf, rbuf, fbuf,
    mloc, mall, out_t, cnt_t, cnt_o, obuf, st1, wh, wl, y2, z2, zz, abuf, asbuf,
    win_sem, ml_sem, halo_s, halo_r, meta_s, meta_r, bulk_s, bulk_r,
    st1_s, st1_r, st2_s, st2_r, out_sem, fin_sem,
):
    d = lax.axis_index("date")
    s = lax.axis_index("strip")

    bar = pltpu.get_barrier_semaphore()
    for k in range(1, ND):
        pl.semaphore_signal(bar, inc=1, device_id=((d + k) % ND, s), device_id_type=MESH)
    for k in range(1, NS):
        pl.semaphore_signal(bar, inc=1, device_id=(d, (s + k) % NS), device_id_type=MESH)

    def window(g):
        lo, hi = max(8 * g - 8, 0), min(8 * g + 16, R)
        at = lo - (8 * g - 8)
        return pltpu.make_async_copy(
            stack.at[:, lo:hi, :], win.at[g, :, at : at + hi - lo, :], win_sem.at[g]
        )

    order = [(i + 1) % G for i in range(G)]
    for g in order:
        window(g).start()
    metas = [
        pltpu.make_async_copy(ref, mloc.at[i], ml_sem.at[i])
        for i, ref in enumerate((ftile, frow, fcount, fowner))
    ]
    for cp in metas:
        cp.start()

    total = spat[0]
    for k in range(1, 2 * RAD + 1):
        total = total + spat[k]
    tot = jnp.full((8, CB), total, F32)
    scale = 1.0 / (tot * tot)
    for q in range(CB // 8):
        row = iota((8, CB), 0) + 8 * q
        col = iota((8, CB), 1)
        main = row - col + RAD
        edge = jnp.where(row < 128, row - 128, row + 128) - col + RAD
        vm, ve = jnp.zeros((8, CB), F32), jnp.zeros((8, CB), F32)
        has_edge = 120 <= 8 * q < 136
        for k in range(2 * RAD + 1):
            vm = jnp.where(main == k, spat[k], vm)
            if has_edge:
                ve = jnp.where(edge == k, spat[k], ve)
        fbuf[q] = vm * scale
        fbuf[32 + q] = ve * scale
    h, l = split(fbuf[0:32].reshape(CB, CB))
    b0h[...], b0l[...] = h, l
    h, l = split(fbuf[32:64].reshape(CB, CB))
    b1h[...], b1l[...] = h, l
    rp[0] = jnp.zeros((TL, 8, CB), F32)
    rp[ND + 1] = jnp.zeros((TL, 8, CB), F32)

    def filter_chunk(g):
        def row_pass(t, carry):
            for p in range(ND):
                cols = slice(p * CB, (p + 1) * CB)
                acc = spat[0] * win[g, t, 2:10, cols]
                for k in range(1, 2 * RAD + 1):
                    acc = acc + spat[k] * win[g, t, 2 + k : 10 + k, cols]
                rp[p + 1, t] = acc
            return carry

        lax.fori_loop(0, TL, row_pass, 0)
        x = rp[1 : ND + 1].reshape(ND * TL * 8, CB)
        xh, xl = split(x)
        low = dot(xh, b0h[...]) + dot(xl, b0h[...]) + dot(xh, b0l[...])
        e = jnp.concatenate([rp[0:ND, :, :, 128:], rp[2 : ND + 2, :, :, :128]], axis=-1)
        eh, el = split(e.reshape(ND * TL * 8, CB))
        low = low + dot(eh, b1h[...]) + dot(el, b1h[...]) + dot(eh, b1l[...])
        low = low.reshape(ND, TL, 8, CB)
        for p in range(ND):
            sbuf[p, g] = win[g, :, 8:16, p * CB : (p + 1) * CB] - low[p]
        rbuf[g, pl.ds(TL * d, TL)] = sbuf[d, g]

    def bulk(g, k):
        p = (d + k) % ND
        return pltpu.make_async_remote_copy(
            src_ref=sbuf.at[p, g],
            dst_ref=rbuf.at[g, pl.ds(TL * d, TL)],
            send_sem=bulk_s.at[g, k],
            recv_sem=bulk_r.at[g, k],
            device_id=(p, s),
            device_id_type=MESH,
        )

    def send_chunk(g):
        for k in range(1, ND):
            bulk(g, k).start()

    def halo(down):
        src = stack.at[:, R - 8 : R, :] if down else stack.at[:, 0:8, :]
        dst = win.at[0, :, 0:8, :] if down else win.at[G - 1, :, 16:24, :]
        i = 0 if down else 1
        to = (s + 1) % NS if down else (s + NS - 1) % NS
        return pltpu.make_async_remote_copy(
            src_ref=src, dst_ref=dst, send_sem=halo_s.at[i], recv_sem=halo_r.at[i],
            device_id=(d, to), device_id_type=MESH,
        )

    def meta(k):
        return pltpu.make_async_remote_copy(
            src_ref=mloc, dst_ref=mall.at[d], send_sem=meta_s.at[k], recv_sem=meta_r.at[k],
            device_id=((d + k) % ND, s), device_id_type=MESH,
        )

    def wait_window(g):
        pltpu.make_async_copy(stack.at[:, 0:24, :], win.at[g], win_sem.at[g]).wait()

    wait_window(order[0])
    filter_chunk(order[0])
    pl.semaphore_wait(bar, ND - 1 + NS - 1)
    send_chunk(order[0])
    halo(True).start()
    halo(False).start()
    for cp in metas:
        cp.wait()
    for k in range(1, ND):
        meta(k).start()

    def interior(g, carry):
        wait_window(g)
        filter_chunk(g)
        send_chunk(g)
        return carry

    lax.fori_loop(2, G - 1, interior, 0)

    r_, c_ = iota((T, T), 0), iota((T, T), 1)
    r2, c2 = iota((T, 2 * T), 0), iota((T, 2 * T), 1) % T
    near = jnp.where(r_ == c_, 1.0, 0.0).astype(F32)
    far = jnp.where(r2 == c2, 1.0, 0.0).astype(F32)
    for k in range(5):
        near = near - jnp.where(r_ - c_ == k - 2, temp[0, k], 0.0)
        far = far - jnp.where(r2 - c2 == 8 * (k - 2), temp[1, k], 0.0)
    tt = jnp.dot(near, far, precision=lax.Precision.HIGHEST, preferred_element_type=F32)
    wh[...] = jnp.zeros(wh.shape, BF16)
    wl[...] = jnp.zeros(wl.shape, BF16)
    half = iota((8, 2 * T), 1) < T
    for i in range(ND):
        part = tt[8 * i : 8 * i + 8]
        base = jnp.concatenate([jnp.where(half, part, 0.0), jnp.where(half, 0.0, part)], axis=0)
        bh, bl = split(base)
        for p in range(ND):
            wh[i * 128 + 16 * p : i * 128 + 16 * p + 16, 128 * p : 128 * p + 128] = bh
            wl[i * 128 + 16 * p : i * 128 + 16 * p + 16, 128 * p : 128 * p + 128] = bl

    halo(True).wait()
    halo(False).wait()
    for g in (0, G - 1):
        window(g).wait()

    @pl.when(s == 0)
    def _():
        win[0, :, 0:8, :] = jnp.zeros((TL, 8, C), F32)

    @pl.when(s == NS - 1)
    def _():
        win[G - 1, :, 16:24, :] = jnp.zeros((TL, 8, C), F32)

    def edge_chunk(i, carry):
        filter_chunk((G - 1) * i)
        return carry

    lax.fori_loop(0, 2, edge_chunk, 0)

    mall[d] = mloc[...]
    for k in range(1, ND):
        meta(k).wait()
    cnt_t[...] = jnp.zeros(cnt_t.shape, F32)

    def block(p, carry):
        tile, row, count, owner = (mall[p, i] for i in range(4))
        jj = iota((CB, F), 0)
        inside = ((jj >> 7) == tile) & ((jj & 127) < count)
        m = jnp.where(inside, 1.0, 0.0).astype(BF16)
        xh, xl = split(sbuf[p].reshape(G * TL * 8, CB))
        g_ = (dot(xh, m) + dot(xl, m)).reshape(G, TL, 8, F)
        here = iota((G, 8, F), 0) * 8 + iota((G, 8, F), 1) == row.reshape(1, 1, F)
        picked = jnp.sum(jnp.where(here[:, None], g_, 0.0), axis=0)
        cf = count.astype(F32)
        mean = jnp.sum(picked, axis=1) / cf
        own = jnp.broadcast_to(owner.astype(F32), (F, F))
        own_t = own.T
        sub, lane = iota((F, F), 0), iota((F, F), 1)
        earlier = (own == own_t) & (sub < lane)
        slot = jnp.sum(jnp.where(earlier, 1.0, 0.0), axis=0, keepdims=True)
        onehot = jnp.where(own_t == lane.astype(F32), 1.0, 0.0)
        rows = jnp.concatenate(
            [
                jnp.where(slot == 0.0, mean, 0.0),
                jnp.where(slot == 1.0, mean, 0.0),
                jnp.where(iota((8, F), 0).astype(F32) == slot, cf, 0.0),
            ],
            axis=0,
        )
        got = jnp.dot(rows, onehot, precision=lax.Precision.HIGHEST, preferred_element_type=F32)
        out_t[pl.ds(pl.multiple_of(16 * p, 16), 16)] = got[0:16]
        cnt_t[pl.ds(pl.multiple_of(8 * p, 8), 8)] = got[16:24]
        return carry

    lax.fori_loop(0, ND, block, 0)
    obuf[...] = out_t[...].T
    cnt_o[...] = cnt_t[...].T

    def stage1(k):
        p = (d + k) % ND
        return pltpu.make_async_remote_copy(
            src_ref=obuf.at[pl.ds(pl.multiple_of(16 * p, 16), 16)], dst_ref=st1.at[d],
            send_sem=st1_s.at[k], recv_sem=st1_r.at[k],
            device_id=(p, s), device_id_type=MESH,
        )

    for k in range(1, ND):
        stage1(k).start()
    mine = pl.ds(pl.multiple_of(16 * d, 16), 16)
    st1[d] = obuf[mine]
    send_chunk(0)
    send_chunk(G - 1)

    ca = [-temp[0, k] for k in range(5)]
    cb = [-temp[1, k] for k in range(5)]
    ca[2], cb[2] = 1.0 + ca[2], 1.0 + cb[2]

    def finish_chunk(g):
        for k in range(1, ND):
            bulk(g, k).wait()

        def level(src, dst, coef, step):
            for t in range(T):
                acc = coef[2] * src(t)
                for k in (0, 1, 3, 4):
                    u = t + step * (k - 2)
                    if 0 <= u < T:
                        acc = acc + coef[k] * src(u)
                dst(t, acc)

        def put_f(t, v):
            fbuf[t] = v

        def put_r(t, v):
            rbuf[g, t] = v

        level(lambda t: rbuf[g, t], put_f, ca, 1)
        level(lambda t: fbuf[t], put_r, cb, 8)
        result(g).start()

    def result(g):
        return pltpu.make_async_copy(
            rbuf.at[g],
            res_out.at[:, pl.ds(pl.multiple_of(8 * g, 8), 8), :],
            out_sem.at[g],
        )

    def finish(g, carry):
        finish_chunk(g)
        return carry

    lax.fori_loop(1, G - 1, finish, 0)

    for k in range(1, ND):
        stage1(k).wait()
    ser = jnp.concatenate([st1[i] for i in range(ND)], axis=-1)
    sh, sl = split(ser)
    y = dot(sh, wh[...]) + dot(sl, wh[...]) + dot(sh, wl[...])
    cnt = cnt_o[mine]
    for i in range(NS):
        y2[i, :, 0 : 8 * F] = y[i : i + 1]
        y2[i, :, 8 * F : 9 * F] = cnt[i : i + 1]

    def stage2(k):
        o = (s + k) % NS
        return pltpu.make_async_remote_copy(
            src_ref=y2.at[o], dst_ref=z2.at[s],
            send_sem=st2_s.at[k], recv_sem=st2_r.at[k],
            device_id=(d, o), device_id_type=MESH,
        )

    for k in range(1, NS):
        stage2(k).start()
    z2[s] = y2[s]

    lax.fori_loop(0, 1, finish, 0)

    for k in range(1, NS):
        stage2(k).wait()
    for i in range(NS):
        zz[i : i + 1] = z2[i]
    z, cn = zz[:, 0 : 8 * F], zz[:, 8 * F : 9 * F]
    spread = jnp.where(
        iota((F, 8 * F), 0) == (iota((F, 8 * F), 1) // F) * 8 + (iota((F, 8 * F), 1) % F) // T, 1.0, 0.0
    ).astype(BF16)
    weight = dot(cn.astype(BF16), spread)
    part = jnp.sum(weight * z, axis=0, keepdims=True)
    acc = part[:, 0:F]
    for i in range(1, ND):
        acc = acc + part[:, i * F : (i + 1) * F]
    acc = acc + jnp.concatenate([acc[:, T:], acc[:, :T]], axis=1)
    asset = acc / jnp.sum(cn)
    for i in range(ND):
        cols = slice(i * F, (i + 1) * F)
        abuf[16 * i : 16 * i + 16] = jnp.where(weight[:, cols] > 0, z[:, cols] - asset, 0.0)
    asbuf[...] = asset
    ends = [
        pltpu.make_async_copy(abuf, anom_out, fin_sem.at[0]),
        pltpu.make_async_copy(asbuf, asset_out, fin_sem.at[1]),
    ]
    for cp in ends:
        cp.start()

    lax.fori_loop(G - 1, G, finish, 0)
    for cp in ends:
        cp.wait()
    for g in range(G):
        result(g).wait()


def shards(stack, spatial_taps, temporal_taps, foot_tile, foot_row, foot_count, foot_owner):
    anywhere, smem = pl.BlockSpec(memory_space=pl.ANY), pl.BlockSpec(memory_space=pltpu.SMEM)
    vm, dma = pltpu.VMEM, pltpu.SemaphoreType.DMA
    scratch = [
        vm((G, TL, 24, C), F32), vm((ND + 2, TL, 8, CB), F32),
        vm((CB, CB), BF16), vm((CB, CB), BF16), vm((CB, CB), BF16), vm((CB, CB), BF16),
        vm((ND, G, TL, 8, CB), F32), vm((G, T, 8, CB), F32), vm((T, 8, CB), F32),
        vm((4, 1, F), I32), vm((ND, 4, 1, F), I32),
        vm((F, F), F32), vm((F, F), F32), vm((F, F), F32), vm((F, F), F32),
        vm((ND, NS, F), F32), vm((8 * F, 8 * F), BF16), vm((8 * F, 8 * F), BF16),
        vm((NS, 1, 9 * F), F32), vm((NS, 1, 9 * F), F32), vm((NS, 9 * F), F32),
        vm((F, F), F32), vm((1, F), F32),
        dma((G,)), dma((4,)), dma((2,)), dma((2,)), dma((ND,)), dma((ND,)),
        dma((G, ND)), dma((G, ND)), dma((ND,)), dma((ND,)), dma((NS,)), dma((NS,)),
        dma((G,)), dma((2,)),
    ]
    residual, anomaly, asset = pl.pallas_call(
        kernel,
        out_shape=(
            jax.ShapeDtypeStruct((T, R, CB), F32),
            jax.ShapeDtypeStruct((F, F), F32),
            jax.ShapeDtypeStruct((1, F), F32),
        ),
        in_specs=[anywhere, smem, smem, anywhere, anywhere, anywhere, anywhere],
        out_specs=(anywhere, anywhere, anywhere),
        scratch_shapes=scratch,
        compiler_params=pltpu.CompilerParams(
            collective_id=0, has_side_effects=True, vmem_limit_bytes=60 << 20
        ),
        name="series",
    )(
        stack, spatial_taps, temporal_taps, foot_tile.reshape(1, F), foot_row.reshape(1, F),
        foot_count.reshape(1, F), foot_owner.reshape(1, F),
    )
    return residual, anomaly.reshape(1, 2 * F, T), asset[:, :T]


def solution(mesh):
    rows = P(("date", "strip"))
    return jax.shard_map(
        shards,
        mesh=mesh,
        in_specs=(P("date", "strip", None), P(), P(), rows, rows, rows, P(("date", "strip"), None)),
        out_specs=(P(None, "strip", "date"), P(("date", "strip"), None, None), P(("date", "strip"), None)),
        check_vma=False,
    )
```

time: 281 us -> 68.4 us (0.24)
  other arithmetic: 118 us -> 0 us
  waiting for transfers between devices: 65.9 us -> 0 us
  Pallas kernels: 0 us -> 60.7 us
  local copies, waits for them, and re-layouts: 62.2 us -> 6.85 us
  starting transfers between devices: 32.2 us -> 0 us
    pallas_call x0 -> x1, Pallas kernels: none -> 60.7 us  [shards(): pl.pallas_call(kernel, out_shape=(jax.ShapeDtypeStruct((T, R, CB), F32),...]
    all_to_all x3 -> x0, waiting for transfers between devices: 55.8 us -> none  [the longest x1 46.9 us: shards(): lax.all_to_all(corrected, 'date', split_axis=2, concat_axis=0, tiled=True)]
    sub x3 -> x0, other arithmetic: 51.7 us -> none  [the longest x1 32.9 us: shards(): corrected = stack - taps_pass(rimmed, weights, 1, stack.shape[1])]
    add x1 -> x0, other arithmetic: 42 us -> none  [taps_pass(): summed + weights[k] * lax.slice_in_dim(padded, k, k + length, axis=axis_num)]
    all_to_all x3 -> x0, starting transfers between devices: 26.8 us -> none  [the longest x1 10.6 us: shards(): lax.all_to_all(out_weight.reshape(devices_all, PAIR_CAP), ('date', 'strip...]
    unnamed x16 -> x5, local copies, waits for them, and re-layouts: 26.8 us -> 5.93 us
    all_to_all x2 -> x0, other arithmetic: 14.6 us -> none  [the longest x1 13.8 us: shards(): lax.all_to_all(corrected, 'date', split_axis=2, concat_axis=0, tiled=True)]
    reshape x2 -> x1, local copies, waits for them, and re-layouts: 12.3 us -> 0.92 us  [shards(): return (residual, anomaly.reshape(1, 2 * F, T), asset[:, :T])]
  transfers between devices with their start and end apart: 5 -> 0, of which waited for: 4 -> 0; matrix products, arithmetic and copies ran while one was open for 26% -> 0% of each run, Pallas kernels for 0% -> 0%
where the time goes in v1:
time: 68.4 us; the launch traced here: 68.2 us
  Pallas kernels  60.7 us (89%)
  local copies, waits for them, and re-layouts  6.85 us (10%)
    pallas_call x1, Pallas kernels, shards(): pl.pallas_call(kernel, out_shape=(jax.ShapeDtypeStruct((T, R, CB), F32),...  60.7 us
    unnamed x5, local copies, waits for them, and re-layouts  5.93 us

profile of v1, /device:TPU:1, one launch (start us, length us, event | category | flops | bytes accessed | tf_op | source)
XLA Modules:
  0.0 68.2 jit_solution(4068696560401228237)
XLA Ops:
  0.6 60.7 %series.1 = (f32[64,64,256]{2,1,0:T(8,128)}, f32[128,128]{1,0:T(8,128)}, f32[1,128]{1,0:T(1,128)}) custom-call(f32[8,64,2048]{2,1,0:T(8,128)} %stack.1, f32[13]{0:T(128)} %spat.1, f32[2,5]{1,0:T(2,128)} %temp.1, s32[1,128]{1,0:T(1,128)} %bitcast.5, s32[1,128]{1,0:T(1,128)} %bitcast.6, s32[1,128]{1,0:T(1,128)} %bitcast.7, s32[1,128]{1,0:T(1,128)} %bitcast.8), custom_call_target="tpu_custom_call" | custom-call | tf_op jit(solution)/shard_map/series/pallas_call | solution.py:372
  61.4 0.9 %reshape.25 = f32[1,256,64]{2,1,0:T(8,128)S(1)} reshape(f32[128,128]{1,0:T(8,128)} %get-tuple-element.7) | data formatting | bytes 131072 | tf_op jit(solution)/shard_map/reshape | solution.py:390
  62.3 0.7 %copy.11 = f32[1,256,64]{1,2,0:T(8,128)} copy(f32[1,256,64]{2,1,0:T(8,128)S(1)} %reshape.25) | data formatting | bytes 131072
  63.0 0.0 copy-start
  63.0 4.7 %copy.14 = f32[64,64,256]{2,1,0:T(8,128)} copy(f32[64,64,256]{2,1,0:T(8,128)} %get-tuple-element.18) | data formatting | bytes 8388608
  67.7 0.0 copy-done
  67.7 0.5 copy.15
Async XLA Ops:
  63.0 4.7 %copy-start = (f32[1,128]{1,0:T(1,128)S(1)}, f32[1,128]{1,0:T(1,128)}, u32[]{:S(2)}) copy-start(f32[1,128]{1,0:T(1,128)} %get-tuple-element.8) | copy-start | bytes 1540

commit v2 on v1

--- a/solution.py
+++ b/solution.py
@@ -30,13 +30,27 @@
     return lax.broadcasted_iota(I32, shape, dim)
 
 
+def filter_dates(src, mid, dst, temp):
+    ca = [-temp[0, k] for k in range(5)]
+    cb = [-temp[1, k] for k in range(5)]
+    ca[2], cb[2] = 1.0 + ca[2], 1.0 + cb[2]
+    for a, b, coef, step in ((src, mid, ca, 1), (mid, dst, cb, 8)):
+        for t in range(T):
+            acc = coef[2] * a[t]
+            for k in (0, 1, 3, 4):
+                u = t + step * (k - 2)
+                if 0 <= u < T:
+                    acc = acc + coef[k] * a[u]
+            b[t] = acc
+
+
 def kernel(
     stack, spat, temp, ftile, frow, fcount, fowner,
-    res_out, anom_out, asset_out,
+    gat_out, anom_out, asset_out,
     win, rp, b0h, b0l, b1h, b1l, sbuf, rbuf, fbuf,
-    mloc, mall, out_t, cnt_t, cnt_o, obuf, st1, wh, wl, y2, z2, zz, abuf, asbuf,
+    mloc, mall, out_t, cnt_t, cnt_o, obuf, st1, wh, wl, y2, z2, zz, xbuf, abuf, asbuf,
     win_sem, ml_sem, halo_s, halo_r, meta_s, meta_r, bulk_s, bulk_r,
-    st1_s, st1_r, st2_s, st2_r, out_sem, fin_sem,
+    st1_s, st1_r, st2_s, st2_r, keep_sem, out_sem, fin_sem,
 ):
     d = lax.axis_index("date")
     s = lax.axis_index("strip")
@@ -109,22 +123,26 @@
         low = low.reshape(ND, TL, 8, CB)
         for p in range(ND):
             sbuf[p, g] = win[g, :, 8:16, p * CB : (p + 1) * CB] - low[p]
-        rbuf[g, pl.ds(TL * d, TL)] = sbuf[d, g]
-
-    def bulk(g, k):
+
+    def bulk(g, k, into=rbuf):
         p = (d + k) % ND
         return pltpu.make_async_remote_copy(
             src_ref=sbuf.at[p, g],
-            dst_ref=rbuf.at[g, pl.ds(TL * d, TL)],
+            dst_ref=into.at[g, pl.ds(TL * d, TL)],
             send_sem=bulk_s.at[g, k],
             recv_sem=bulk_r.at[g, k],
             device_id=(p, s),
             device_id_type=MESH,
         )
 
-    def send_chunk(g):
+    def send_chunk(g, into=rbuf):
         for k in range(1, ND):
-            bulk(g, k).start()
+            bulk(g, k, into).start()
+
+    def keep(g, into=rbuf):
+        return pltpu.make_async_copy(
+            sbuf.at[d, g], into.at[g, pl.ds(TL * d, TL)], keep_sem.at[g]
+        )
 
     def halo(down):
         src = stack.at[:, R - 8 : R, :] if down else stack.at[:, 0:8, :]
@@ -254,44 +272,20 @@
     mine = pl.ds(pl.multiple_of(16 * d, 16), 16)
     st1[d] = obuf[mine]
     send_chunk(0)
-    send_chunk(G - 1)
-
-    ca = [-temp[0, k] for k in range(5)]
-    cb = [-temp[1, k] for k in range(5)]
-    ca[2], cb[2] = 1.0 + ca[2], 1.0 + cb[2]
-
-    def finish_chunk(g):
+    send_chunk(G - 1, gat_out)
+    for g in range(G - 1):
+        keep(g).start()
+    keep(G - 1, gat_out).start()
+
+    def result(g):
+        return pltpu.make_async_copy(rbuf.at[g], gat_out.at[g], out_sem.at[g])
+
+    def finish(g, carry):
+        keep(g).wait()
         for k in range(1, ND):
             bulk(g, k).wait()
-
-        def level(src, dst, coef, step):
-            for t in range(T):
-                acc = coef[2] * src(t)
-                for k in (0, 1, 3, 4):
-                    u = t + step * (k - 2)
-                    if 0 <= u < T:
-                        acc = acc + coef[k] * src(u)
-                dst(t, acc)
-
-        def put_f(t, v):
-            fbuf[t] = v
-
-        def put_r(t, v):
-            rbuf[g, t] = v
-
-        level(lambda t: rbuf[g, t], put_f, ca, 1)
-        level(lambda t: fbuf[t], put_r, cb, 8)
+        filter_dates(rbuf.at[g], fbuf, rbuf.at[g], temp)
         result(g).start()
-
-    def result(g):
-        return pltpu.make_async_copy(
-            rbuf.at[g],
-            res_out.at[:, pl.ds(pl.multiple_of(8 * g, 8), 8), :],
-            out_sem.at[g],
-        )
-
-    def finish(g, carry):
-        finish_chunk(g)
         return carry
 
     lax.fori_loop(1, G - 1, finish, 0)
@@ -337,7 +331,10 @@
     asset = acc / jnp.sum(cn)
     for i in range(ND):
         cols = slice(i * F, (i + 1) * F)
-        abuf[16 * i : 16 * i + 16] = jnp.where(weight[:, cols] > 0, z[:, cols] - asset, 0.0)
+        anom = jnp.where(weight[:, cols] > 0, z[:, cols] - asset, 0.0)
+        xbuf[pl.ds(32 * i, NS, stride=2)] = anom
+        xbuf[pl.ds(32 * i + 1, NS, stride=2)] = pltpu.roll(anom, T, 1)
+    abuf[...] = xbuf[...].T[0:T]
     asbuf[...] = asset
     ends = [
         pltpu.make_async_copy(abuf, anom_out, fin_sem.at[0]),
@@ -345,8 +342,33 @@
     ]
     for cp in ends:
         cp.start()
-
-    lax.fori_loop(G - 1, G, finish, 0)
+    for cp in ends:
+        cp.wait()
+    for g in range(G - 1):
+        result(g).wait()
+    keep(G - 1, gat_out).wait()
+    for k in range(1, ND):
+        bulk(G - 1, k, gat_out).wait()
+
+
+def finish_kernel(gat, anom, asset, temp, res_out, anom_out, asset_out, xb, fb, in_sem, out_sem, fin_sem):
+    def result(g):
+        src = gat.at[g] if g < G - 1 else xb
+        return pltpu.make_async_copy(src, res_out.at[:, 8 * g : 8 * g + 8, :], out_sem.at[g])
+
+    last = pltpu.make_async_copy(gat.at[G - 1], xb, in_sem)
+    last.start()
+    for g in range(G - 1):
+        result(g).start()
+    ends = [
+        pltpu.make_async_copy(anom, anom_out, fin_sem.at[0]),
+        pltpu.make_async_copy(asset, asset_out, fin_sem.at[1]),
+    ]
+    for cp in ends:
+        cp.start()
+    last.wait()
+    filter_dates(xb, fb, xb, temp)
+    result(G - 1).start()
     for cp in ends:
         cp.wait()
     for g in range(G):
@@ -355,6 +377,7 @@
 
 def shards(stack, spatial_taps, temporal_taps, foot_tile, foot_row, foot_count, foot_owner):
     anywhere, smem = pl.BlockSpec(memory_space=pl.ANY), pl.BlockSpec(memory_space=pltpu.SMEM)
+    hbm = pl.BlockSpec(memory_space=pltpu.HBM)
     vm, dma = pltpu.VMEM, pltpu.SemaphoreType.DMA
     scratch = [
         vm((G, TL, 24, C), F32), vm((ND + 2, TL, 8, CB), F32),
@@ -364,30 +387,47 @@
         vm((F, F), F32), vm((F, F), F32), vm((F, F), F32), vm((F, F), F32),
         vm((ND, NS, F), F32), vm((8 * F, 8 * F), BF16), vm((8 * F, 8 * F), BF16),
         vm((NS, 1, 9 * F), F32), vm((NS, 1, 9 * F), F32), vm((NS, 9 * F), F32),
-        vm((F, F), F32), vm((1, F), F32),
+        vm((2 * F, F), F32), vm((T, 2 * F), F32), vm((1, F), F32),
         dma((G,)), dma((4,)), dma((2,)), dma((2,)), dma((ND,)), dma((ND,)),
         dma((G, ND)), dma((G, ND)), dma((ND,)), dma((ND,)), dma((NS,)), dma((NS,)),
-        dma((G,)), dma((2,)),
+        dma((G,)), dma((G,)), dma((2,)),
     ]
-    residual, anomaly, asset = pl.pallas_call(
+    held = [
+        pltpu.with_memory_space_constraint(a, pltpu.HBM)
+        for a in (
+            stack, spatial_taps, temporal_taps, foot_tile.reshape(1, F), foot_row.reshape(1, F),
+            foot_count.reshape(1, F), foot_owner.reshape(1, F),
+        )
+    ]
+    gathered, anomaly, asset = pl.pallas_call(
         kernel,
         out_shape=(
-            jax.ShapeDtypeStruct((T, R, CB), F32),
-            jax.ShapeDtypeStruct((F, F), F32),
+            jax.ShapeDtypeStruct((G, T, 8, CB), F32),
+            jax.ShapeDtypeStruct((T, 2 * F), F32),
             jax.ShapeDtypeStruct((1, F), F32),
         ),
-        in_specs=[anywhere, smem, smem, anywhere, anywhere, anywhere, anywhere],
+        in_specs=[hbm, smem, smem, anywhere, anywhere, anywhere, anywhere],
         out_specs=(anywhere, anywhere, anywhere),
         scratch_shapes=scratch,
         compiler_params=pltpu.CompilerParams(
-            collective_id=0, has_side_effects=True, vmem_limit_bytes=60 << 20
+            collective_id=0, has_side_effects=True, vmem_limit_bytes=44 << 20
         ),
         name="series",
-    )(
-        stack, spatial_taps, temporal_taps, foot_tile.reshape(1, F), foot_row.reshape(1, F),
-        foot_count.reshape(1, F), foot_owner.reshape(1, F),
-    )
-    return residual, anomaly.reshape(1, 2 * F, T), asset[:, :T]
+    )(*held)
+    residual, anomaly, asset = pl.pallas_call(
+        finish_kernel,
+        out_shape=(
+            jax.ShapeDtypeStruct((T, R, CB), F32),
+            jax.ShapeDtypeStruct((T, 2 * F), F32),
+            jax.ShapeDtypeStruct((1, F), F32),
+        ),
+        in_specs=[anywhere, anywhere, anywhere, smem],
+        out_specs=(hbm, hbm, hbm),
+        scratch_shapes=[vm((T, 8, CB), F32), vm((T, 8, CB), F32), dma, dma((G,)), dma((2,))],
+        compiler_params=pltpu.CompilerParams(vmem_limit_bytes=4 << 20),
+        name="finish",
+    )(gathered, anomaly, asset, temporal_taps)
+    return residual, anomaly.T[None], asset[:, :T]
 
 
 def solution(mesh):

time: 68.4 us -> 63.1 us (0.923)
  local copies, waits for them, and re-layouts: 6.85 us -> 0.01 us
  Pallas kernels: 60.7 us -> 62.3 us
    unnamed x5 -> x2, local copies, waits for them, and re-layouts: 5.93 us -> 0.01 us
    pallas_call x1 -> x2, Pallas kernels: 60.7 us -> 62.3 us  [the longest x1 59.6 us: shards(): pl.pallas_call(kernel, out_shape=(jax.ShapeDtypeStruct((G, T, 8, CB), F32...]
    reshape x1 -> x0, local copies, waits for them, and re-layouts: 0.92 us -> none  [shards(): return (residual, anomaly.reshape(1, 2 * F, T), asset[:, :T])]
where the time goes in v2:
time: 63.1 us; the launch traced here: 63 us
  Pallas kernels  62.3 us (99%)
  between operations  0.66 us (1%)
    pallas_call x1, Pallas kernels, shards(): pl.pallas_call(kernel, out_shape=(jax.ShapeDtypeStruct((G, T, 8, CB), F32...  59.6 us
    pallas_call x1, Pallas kernels, shards(): pl.pallas_call(finish_kernel, out_shape=(jax.ShapeDtypeStruct((T, R, CB),...  2.71 us

profile of v2, /device:TPU:1, one launch (start us, length us, event | category | flops | bytes accessed | tf_op | source)
XLA Modules:
  0.0 63.0 jit_solution(8067430787529640723)
XLA Ops:
  0.6 0.0 copy-start
  0.6 59.6 %series.1 = (f32[8,64,8,256]{3,2,1,0:T(8,128)S(1)}, f32[64,256]{1,0:T(8,128)S(1)}, f32[1,128]{1,0:T(1,128)S(1)}) custom-call(f32[8,64,2048]{2,1,0:T(8,128)} %stack.1, f32[13]{0:T(128)} %spat.1, f32[2,5]{1,0:T(2,128)} %temp.3, s32[1,128]{1,0:T(1,128)} %bitcast.8, s32[1,128]{1,0:T(1,128)} %bitcast.9, s32[1,128]{1,0:T(1,128)} %bitcast.10, s32[1,128]{1,0:T(1,128)} %bitcast.11), custom_call_target="tpu_custom_call" | custom-call | tf_op jit(solution)/shard_map/series/pallas_call | solution.py:402
  60.3 0.0 copy-done
  60.3 2.7 %finish.1 = (f32[64,64,256]{2,1,0:T(8,128)}, f32[64,256]{1,0:T(8,128)}, f32[1,128]{1,0:T(1,128)}) custom-call(f32[8,64,8,256]{3,2,1,0:T(8,128)S(1)} %get-tuple-element.9.gat, f32[64,256]{1,0:T(8,128)S(1)} %get-tuple-element.10.anom, f32[1,128]{1,0:T(1,128)S(1)} %get-tuple-element.11.asset, f32[2,5]{1,0:T(2,128)S(1)} %copy-done), custom_call_target="tpu_custom_call" | custom-call | tf_op jit(solution)/shard_map/finish/pallas_call | solution.py:417
Async XLA Ops:
  0.6 59.7 %copy-start = (f32[2,5]{1,0:T(2,128)S(1)}, f32[2,5]{1,0:T(2,128)}, u32[]{:S(2)}) copy-start(f32[2,5]{1,0:T(2,128)} %temp.3) | copy-start | bytes 124

commit v3 on v2

--- a/solution.py
+++ b/solution.py
@@ -14,7 +14,7 @@
 C, CB = 2048, 256
 F = 128
 RAD = 6
-HELD = 2
+HT = 4
 
 
 def dot(a, b):
@@ -50,7 +50,7 @@
     win, rp, b0h, b0l, b1h, b1l, sbuf, rbuf, fbuf,
     mloc, mall, out_t, cnt_t, cnt_o, obuf, st1, wh, wl, y2, z2, zz, xbuf, abuf, asbuf,
     win_sem, ml_sem, halo_s, halo_r, meta_s, meta_r, bulk_s, bulk_r,
-    st1_s, st1_r, st2_s, st2_r, keep_sem, out_sem, fin_sem,
+    st1_s, st1_r, st2_s, st2_r, keep_sem, out_sem, fin_sem, group_in, all_in,
 ):
     d = lax.axis_index("date")
     s = lax.axis_index("strip")
@@ -58,8 +58,11 @@
     bar = pltpu.get_barrier_semaphore()
     for k in range(1, ND):
         pl.semaphore_signal(bar, inc=1, device_id=((d + k) % ND, s), device_id_type=MESH)
-    for k in range(1, NS):
-        pl.semaphore_signal(bar, inc=1, device_id=(d, (s + k) % NS), device_id_type=MESH)
+
+    @pl.when(d == 0)
+    def _():
+        for k in range(1, NS):
+            pl.semaphore_signal(bar, inc=1, device_id=(0, (s + k) % NS), device_id_type=MESH)
 
     def window(g):
         lo, hi = max(8 * g - 8, 0), min(8 * g + 16, R)
@@ -68,8 +71,16 @@
             stack.at[:, lo:hi, :], win.at[g, :, at : at + hi - lo, :], win_sem.at[g]
         )
 
+    def early(h):
+        dates = slice(HT * h, HT * h + HT)
+        return pltpu.make_async_copy(
+            stack.at[dates, 0:24, :], win.at[order[0], dates], win_sem.at[G if h else order[0]]
+        )
+
     order = [(i + 1) % G for i in range(G)]
-    for g in order:
+    early(0).start()
+    early(1).start()
+    for g in order[1:]:
         window(g).start()
     metas = [
         pltpu.make_async_copy(ref, mloc.at[i], ml_sem.at[i])
@@ -103,7 +114,10 @@
     rp[0] = jnp.zeros((TL, 8, CB), F32)
     rp[ND + 1] = jnp.zeros((TL, 8, CB), F32)
 
-    def filter_chunk(g):
+    def filter_chunk(g, first=None):
+        t0, nt = (0, TL) if first is None else (first, HT)
+        dates = slice(t0, t0 + nt)
+
         def row_pass(t, carry):
             for p in range(ND):
                 cols = slice(p * CB, (p + 1) * CB)
@@ -113,16 +127,16 @@
                 rp[p + 1, t] = acc
             return carry
 
-        lax.fori_loop(0, TL, row_pass, 0)
-        x = rp[1 : ND + 1].reshape(ND * TL * 8, CB)
+        lax.fori_loop(t0, t0 + nt, row_pass, 0)
+        x = rp[1 : ND + 1, dates].reshape(ND * nt * 8, CB)
         xh, xl = split(x)
         low = dot(xh, b0h[...]) + dot(xl, b0h[...]) + dot(xh, b0l[...])
-        e = jnp.concatenate([rp[0:ND, :, :, 128:], rp[2 : ND + 2, :, :, :128]], axis=-1)
-        eh, el = split(e.reshape(ND * TL * 8, CB))
+        e = jnp.concatenate([rp[0:ND, dates, :, 128:], rp[2 : ND + 2, dates, :, :128]], axis=-1)
+        eh, el = split(e.reshape(ND * nt * 8, CB))
         low = low + dot(eh, b1h[...]) + dot(el, b1h[...]) + dot(eh, b1l[...])
-        low = low.reshape(ND, TL, 8, CB)
+        low = low.reshape(ND, nt, 8, CB)
         for p in range(ND):
-            sbuf[p, g] = win[g, :, 8:16, p * CB : (p + 1) * CB] - low[p]
+            sbuf[p, g, dates] = win[g, dates, 8:16, p * CB : (p + 1) * CB] - low[p]
 
     def bulk(g, k, into=rbuf):
         p = (d + k) % ND
@@ -135,6 +149,21 @@
             device_id_type=MESH,
         )
 
+    def half(h, k):
+        g, p = order[0], (d + k) % ND
+        return pltpu.make_async_remote_copy(
+            src_ref=sbuf.at[p, g, pl.ds(HT * h, HT)],
+            dst_ref=rbuf.at[g, pl.ds(TL * d + HT * h, HT)],
+            send_sem=bulk_s.at[g if h else G, k],
+            recv_sem=bulk_r.at[g if h else G, k],
+            device_id=(p, s),
+            device_id_type=MESH,
+        )
+
+    def send_half(h):
+        for k in range(1, ND):
+            half(h, k).start()
+
     def send_chunk(g, into=rbuf):
         for k in range(1, ND):
             bulk(g, k, into).start()
@@ -163,12 +192,13 @@
     def wait_window(g):
         pltpu.make_async_copy(stack.at[:, 0:24, :], win.at[g], win_sem.at[g]).wait()
 
-    wait_window(order[0])
-    filter_chunk(order[0])
-    pl.semaphore_wait(bar, ND - 1 + NS - 1)
-    send_chunk(order[0])
-    halo(True).start()
-    halo(False).start()
+    early(0).wait()
+    filter_chunk(order[0], 0)
+    pl.semaphore_wait(bar, jnp.where(d == 0, ND - 1 + NS - 1, ND - 1))
+    send_half(0)
+    early(1).wait()
+    filter_chunk(order[0], HT)
+    send_half(1)
     for cp in metas:
         cp.wait()
     for k in range(1, ND):
@@ -180,7 +210,24 @@
         send_chunk(g)
         return carry
 
-    lax.fori_loop(2, G - 1, interior, 0)
+    lax.fori_loop(2, 3, interior, 0)
+
+    @pl.when(d == 0)
+    def _():
+        for k in range(1, NS):
+            pl.semaphore_signal(group_in, inc=1, device_id=(0, (s + k) % NS), device_id_type=MESH)
+        pl.semaphore_wait(group_in, NS - 1)
+        for k in range(1, ND):
+            pl.semaphore_signal(all_in, inc=1, device_id=(k, s), device_id_type=MESH)
+
+    @pl.when(d != 0)
+    def _():
+        pl.semaphore_wait(all_in, 1)
+
+    halo(True).start()
+    halo(False).start()
+
+    lax.fori_loop(3, G - 1, interior, 0)
 
     r_, c_ = iota((T, T), 0), iota((T, T), 1)
     r2, c2 = iota((T, 2 * T), 0), iota((T, 2 * T), 1) % T
@@ -192,10 +239,10 @@
     tt = jnp.dot(near, far, precision=lax.Precision.HIGHEST, preferred_element_type=F32)
     wh[...] = jnp.zeros(wh.shape, BF16)
     wl[...] = jnp.zeros(wl.shape, BF16)
-    half = iota((8, 2 * T), 1) < T
+    left = iota((8, 2 * T), 1) < T
     for i in range(ND):
         part = tt[8 * i : 8 * i + 8]
-        base = jnp.concatenate([jnp.where(half, part, 0.0), jnp.where(half, 0.0, part)], axis=0)
+        base = jnp.concatenate([jnp.where(left, part, 0.0), jnp.where(left, 0.0, part)], axis=0)
         bh, bl = split(base)
         for p in range(ND):
             wh[i * 128 + 16 * p : i * 128 + 16 * p + 16, 128 * p : 128 * p + 128] = bh
@@ -284,11 +331,19 @@
         keep(g).wait()
         for k in range(1, ND):
             bulk(g, k).wait()
+        complete(g)
+        return carry
+
+    def complete(g):
         filter_dates(rbuf.at[g], fbuf, rbuf.at[g], temp)
         result(g).start()
-        return carry
-
-    lax.fori_loop(1, G - 1, finish, 0)
+
+    keep(order[0]).wait()
+    for k in range(1, ND):
+        half(0, k).wait()
+        half(1, k).wait()
+    complete(order[0])
+    lax.fori_loop(2, G - 1, finish, 0)
 
     for k in range(1, ND):
         stage1(k).wait()
@@ -388,9 +443,10 @@
         vm((ND, NS, F), F32), vm((8 * F, 8 * F), BF16), vm((8 * F, 8 * F), BF16),
         vm((NS, 1, 9 * F), F32), vm((NS, 1, 9 * F), F32), vm((NS, 9 * F), F32),
         vm((2 * F, F), F32), vm((T, 2 * F), F32), vm((1, F), F32),
-        dma((G,)), dma((4,)), dma((2,)), dma((2,)), dma((ND,)), dma((ND,)),
-        dma((G, ND)), dma((G, ND)), dma((ND,)), dma((ND,)), dma((NS,)), dma((NS,)),
+        dma((G + 1,)), dma((4,)), dma((2,)), dma((2,)), dma((ND,)), dma((ND,)),
+        dma((G + 1, ND)), dma((G + 1, ND)), dma((ND,)), dma((ND,)), dma((NS,)), dma((NS,)),
         dma((G,)), dma((G,)), dma((2,)),
+        pltpu.SemaphoreType.REGULAR, pltpu.SemaphoreType.REGULAR,
     ]
     held = [
         pltpu.with_memory_space_constraint(a, pltpu.HBM)

time: 63.1 us -> 61.8 us (0.979)
  Pallas kernels: 62.3 us -> 61 us
    pallas_call x1, Pallas kernels: 59.6 us -> 58.3 us  [shards(): pl.pallas_call(kernel, out_shape=(jax.ShapeDtypeStruct((G, T, 8, CB), F32...]
where the time goes in v3:
time: 61.8 us; the launch traced here: 61.6 us
  Pallas kernels  61 us (99%)
  between operations  0.66 us (1%)
    pallas_call x1, Pallas kernels, shards(): pl.pallas_call(kernel, out_shape=(jax.ShapeDtypeStruct((G, T, 8, CB), F32...  58.3 us
    pallas_call x1, Pallas kernels, shards(): pl.pallas_call(finish_kernel, out_shape=(jax.ShapeDtypeStruct((T, R, CB),...  2.71 us

profile of v3, /device:TPU:1, one launch (start us, length us, event | category | flops | bytes accessed | tf_op | source)
XLA Modules:
  0.0 61.6 jit_solution(395649446588381683)
XLA Ops:
  0.6 0.0 copy-start
  0.6 58.3 %series.1 = (f32[8,64,8,256]{3,2,1,0:T(8,128)S(1)}, f32[64,256]{1,0:T(8,128)S(1)}, f32[1,128]{1,0:T(1,128)S(1)}) custom-call(f32[8,64,2048]{2,1,0:T(8,128)} %stack.1, f32[13]{0:T(128)} %spat.1, f32[2,5]{1,0:T(2,128)} %temp.3, s32[1,128]{1,0:T(1,128)} %bitcast.8, s32[1,128]{1,0:T(1,128)} %bitcast.9, s32[1,128]{1,0:T(1,128)} %bitcast.10, s32[1,128]{1,0:T(1,128)} %bitcast.11), custom_call_target="tpu_custom_call" | custom-call | tf_op jit(solution)/shard_map/series/pallas_call | solution.py:458
  58.9 0.0 copy-done
  58.9 2.7 %finish.1 = (f32[64,64,256]{2,1,0:T(8,128)}, f32[64,256]{1,0:T(8,128)}, f32[1,128]{1,0:T(1,128)}) custom-call(f32[8,64,8,256]{3,2,1,0:T(8,128)S(1)} %get-tuple-element.9.gat, f32[64,256]{1,0:T(8,128)S(1)} %get-tuple-element.10.anom, f32[1,128]{1,0:T(1,128)S(1)} %get-tuple-element.11.asset, f32[2,5]{1,0:T(2,128)S(1)} %copy-done), custom_call_target="tpu_custom_call" | custom-call | tf_op jit(solution)/shard_map/finish/pallas_call | solution.py:473
Async XLA Ops:
  0.6 58.3 %copy-start = (f32[2,5]{1,0:T(2,128)S(1)}, f32[2,5]{1,0:T(2,128)}, u32[]{:S(2)}) copy-start(f32[2,5]{1,0:T(2,128)} %temp.3) | copy-start | bytes 124

commit v4 on v3

--- a/solution.py
+++ b/solution.py
@@ -45,11 +45,11 @@
 
 
 def kernel(
-    stack, spat, temp, ftile, frow, fcount, fowner,
+    stack, spat_in, temp_in, ftile, frow, fcount, fowner,
     gat_out, anom_out, asset_out,
-    win, rp, b0h, b0l, b1h, b1l, sbuf, rbuf, fbuf,
+    spat, temp, win, rp, b0h, b0l, b1h, b1l, sbuf, rbuf, fbuf,
     mloc, mall, out_t, cnt_t, cnt_o, obuf, st1, wh, wl, y2, z2, zz, xbuf, abuf, asbuf,
-    win_sem, ml_sem, halo_s, halo_r, meta_s, meta_r, bulk_s, bulk_r,
+    tap_sem, win_sem, ml_sem, halo_s, halo_r, meta_s, meta_r, bulk_s, bulk_r,
     st1_s, st1_r, st2_s, st2_r, keep_sem, out_sem, fin_sem, group_in, all_in,
 ):
     d = lax.axis_index("date")
@@ -78,6 +78,12 @@
         )
 
     order = [(i + 1) % G for i in range(G)]
+    taps = [
+        pltpu.make_async_copy(spat_in, spat, tap_sem.at[0]),
+        pltpu.make_async_copy(temp_in, temp, tap_sem.at[1]),
+    ]
+    for cp in taps:
+        cp.start()
     early(0).start()
     early(1).start()
     for g in order[1:]:
@@ -88,6 +94,9 @@
     ]
     for cp in metas:
         cp.start()
+
+    for cp in taps:
+        cp.wait()
 
     total = spat[0]
     for k in range(1, 2 * RAD + 1):
@@ -196,6 +205,12 @@
     filter_chunk(order[0], 0)
     pl.semaphore_wait(bar, jnp.where(d == 0, ND - 1 + NS - 1, ND - 1))
     send_half(0)
+
+    @pl.when(d == 0)
+    def _():
+        for k in range(1, NS):
+            pl.semaphore_signal(group_in, inc=1, device_id=(0, (s + k) % NS), device_id_type=MESH)
+
     early(1).wait()
     filter_chunk(order[0], HT)
     send_half(1)
@@ -214,12 +229,12 @@
 
     @pl.when(d == 0)
     def _():
-        for k in range(1, NS):
-            pl.semaphore_signal(group_in, inc=1, device_id=(0, (s + k) % NS), device_id_type=MESH)
         pl.semaphore_wait(group_in, NS - 1)
         for k in range(1, ND):
             pl.semaphore_signal(all_in, inc=1, device_id=(k, s), device_id_type=MESH)
 
+    lax.fori_loop(3, 4, interior, 0)
+
     @pl.when(d != 0)
     def _():
         pl.semaphore_wait(all_in, 1)
@@ -227,7 +242,7 @@
     halo(True).start()
     halo(False).start()
 
-    lax.fori_loop(3, G - 1, interior, 0)
+    lax.fori_loop(4, G - 1, interior, 0)
 
     r_, c_ = iota((T, T), 0), iota((T, T), 1)
     r2, c2 = iota((T, 2 * T), 0), iota((T, 2 * T), 1) % T
@@ -406,7 +421,12 @@
         bulk(G - 1, k, gat_out).wait()
 
 
-def finish_kernel(gat, anom, asset, temp, res_out, anom_out, asset_out, xb, fb, in_sem, out_sem, fin_sem):
+def finish_kernel(
+    gat, anom, asset, temp_in, res_out, anom_out, asset_out, temp, xb, fb, in_sem, tap_sem, out_sem, fin_sem
+):
+    taps = pltpu.make_async_copy(temp_in, temp, tap_sem)
+    taps.start()
+
     def result(g):
         src = gat.at[g] if g < G - 1 else xb
         return pltpu.make_async_copy(src, res_out.at[:, 8 * g : 8 * g + 8, :], out_sem.at[g])
@@ -421,6 +441,7 @@
     ]
     for cp in ends:
         cp.start()
+    taps.wait()
     last.wait()
     filter_dates(xb, fb, xb, temp)
     result(G - 1).start()
@@ -431,11 +452,12 @@
 
 
 def shards(stack, spatial_taps, temporal_taps, foot_tile, foot_row, foot_count, foot_owner):
-    anywhere, smem = pl.BlockSpec(memory_space=pl.ANY), pl.BlockSpec(memory_space=pltpu.SMEM)
+    anywhere = pl.BlockSpec(memory_space=pl.ANY)
     hbm = pl.BlockSpec(memory_space=pltpu.HBM)
     vm, dma = pltpu.VMEM, pltpu.SemaphoreType.DMA
+    sm = pltpu.SMEM
     scratch = [
-        vm((G, TL, 24, C), F32), vm((ND + 2, TL, 8, CB), F32),
+        sm((2 * RAD + 1,), F32), sm((2, 5), F32), vm((G, TL, 24, C), F32), vm((ND + 2, TL, 8, CB), F32),
         vm((CB, CB), BF16), vm((CB, CB), BF16), vm((CB, CB), BF16), vm((CB, CB), BF16),
         vm((ND, G, TL, 8, CB), F32), vm((G, T, 8, CB), F32), vm((T, 8, CB), F32),
         vm((4, 1, F), I32), vm((ND, 4, 1, F), I32),
@@ -443,7 +465,7 @@
         vm((ND, NS, F), F32), vm((8 * F, 8 * F), BF16), vm((8 * F, 8 * F), BF16),
         vm((NS, 1, 9 * F), F32), vm((NS, 1, 9 * F), F32), vm((NS, 9 * F), F32),
         vm((2 * F, F), F32), vm((T, 2 * F), F32), vm((1, F), F32),
-        dma((G + 1,)), dma((4,)), dma((2,)), dma((2,)), dma((ND,)), dma((ND,)),
+        dma((2,)), dma((G + 1,)), dma((4,)), dma((2,)), dma((2,)), dma((ND,)), dma((ND,)),
         dma((G + 1, ND)), dma((G + 1, ND)), dma((ND,)), dma((ND,)), dma((NS,)), dma((NS,)),
         dma((G,)), dma((G,)), dma((2,)),
         pltpu.SemaphoreType.REGULAR, pltpu.SemaphoreType.REGULAR,
@@ -462,7 +484,7 @@
             jax.ShapeDtypeStruct((T, 2 * F), F32),
             jax.ShapeDtypeStruct((1, F), F32),
         ),
-        in_specs=[hbm, smem, smem, anywhere, anywhere, anywhere, anywhere],
+        in_specs=[hbm] * 7,
         out_specs=(anywhere, anywhere, anywhere),
         scratch_shapes=scratch,
         compiler_params=pltpu.CompilerParams(
@@ -477,9 +499,11 @@
             jax.ShapeDtypeStruct((T, 2 * F), F32),
             jax.ShapeDtypeStruct((1, F), F32),
         ),
-        in_specs=[anywhere, anywhere, anywhere, smem],
+        in_specs=[anywhere] * 4,
         out_specs=(hbm, hbm, hbm),
-        scratch_shapes=[vm((T, 8, CB), F32), vm((T, 8, CB), F32), dma, dma((G,)), dma((2,))],
+        scratch_shapes=[
+            sm((2, 5), F32), vm((T, 8, CB), F32), vm((T, 8, CB), F32), dma, dma, dma((G,)), dma((2,))
+        ],
         compiler_params=pltpu.CompilerParams(vmem_limit_bytes=4 << 20),
         name="finish",
     )(gathered, anomaly, asset, temporal_taps)

time: 61.8 us -> 58.5 us (0.947)
  Pallas kernels: 61 us -> 57.7 us
    pallas_call x1, Pallas kernels: 58.3 us -> 55.6 us  [shards(): pl.pallas_call(kernel, out_shape=(jax.ShapeDtypeStruct((G, T, 8, CB), F32...]
where the time goes in v4:
time: 58.5 us; the launch traced here: 58.4 us
  Pallas kernels  57.7 us (99%)
  between operations  0.66 us (1%)
    pallas_call x1, Pallas kernels, shards(): pl.pallas_call(kernel, out_shape=(jax.ShapeDtypeStruct((G, T, 8, CB), F32...  55.6 us
    pallas_call x1, Pallas kernels, shards(): pl.pallas_call(finish_kernel, out_shape=(jax.ShapeDtypeStruct((T, R, CB),...  2.17 us

profile of v4, /device:TPU:1, one launch (start us, length us, event | category | flops | bytes accessed | tf_op | source)
XLA Modules:
  0.0 58.4 jit_solution(11457961743372283122)
XLA Ops:
  0.6 0.0 copy-start
  0.6 55.6 %series.1 = (f32[8,64,8,256]{3,2,1,0:T(8,128)S(1)}, f32[64,256]{1,0:T(8,128)S(1)}, f32[1,128]{1,0:T(1,128)S(1)}) custom-call(f32[8,64,2048]{2,1,0:T(8,128)} %stack.1, f32[13]{0:T(128)} %spat_in.1, f32[2,5]{1,0:T(2,128)} %temp_in.3, s32[1,128]{1,0:T(1,128)} %bitcast.8, s32[1,128]{1,0:T(1,128)} %bitcast.9, s32[1,128]{1,0:T(1,128)} %bitcast.10, s32[1,128]{1,0:T(1,128)} %bitcast.11), custom_call_target="tpu_custom_call" | custom-call | tf_op jit(solution)/shard_map/series/pallas_call | solution.py:480
  56.2 0.0 copy-done
  56.2 2.2 %finish.1 = (f32[64,64,256]{2,1,0:T(8,128)}, f32[64,256]{1,0:T(8,128)}, f32[1,128]{1,0:T(1,128)}) custom-call(f32[8,64,8,256]{3,2,1,0:T(8,128)S(1)} %get-tuple-element.9.gat, f32[64,256]{1,0:T(8,128)S(1)} %get-tuple-element.10.anom, f32[1,128]{1,0:T(1,128)S(1)} %get-tuple-element.11.asset, f32[2,5]{1,0:T(2,128)S(1)} %copy-done), custom_call_target="tpu_custom_call" | custom-call | tf_op jit(solution)/shard_map/finish/pallas_call | solution.py:495
Async XLA Ops:
  0.6 55.6 %copy-start = (f32[2,5]{1,0:T(2,128)S(1)}, f32[2,5]{1,0:T(2,128)}, u32[]{:S(2)}) copy-start(f32[2,5]{1,0:T(2,128)} %temp_in.3) | copy-start | bytes 124

commit v5 on v4

--- a/solution.py
+++ b/solution.py
@@ -11,7 +11,7 @@
 ND, NS = 8, 16
 T, TL = 64, 8
 R, G = 64, 8
-C, CB = 2048, 256
+C, CB, NL = 2048, 256, 16
 F = 128
 RAD = 6
 HT = 4
@@ -65,17 +65,24 @@
             pl.semaphore_signal(bar, inc=1, device_id=(0, (s + k) % NS), device_id_type=MESH)
 
     def window(g):
-        lo, hi = max(8 * g - 8, 0), min(8 * g + 16, R)
-        at = lo - (8 * g - 8)
-        return pltpu.make_async_copy(
-            stack.at[:, lo:hi, :], win.at[g, :, at : at + hi - lo, :], win_sem.at[g]
-        )
+        return [
+            pltpu.make_async_copy(
+                stack.at[:, g + j], win.at[g, :, :, 8 + 8 * j : 16 + 8 * j, :], win_sem.at[g, j + 1]
+            )
+            for j in (-1, 0, 1)
+            if 0 <= g + j < G
+        ]
 
     def early(h):
-        dates = slice(HT * h, HT * h + HT)
-        return pltpu.make_async_copy(
-            stack.at[dates, 0:24, :], win.at[order[0], dates], win_sem.at[G if h else order[0]]
-        )
+        dates, g = slice(HT * h, HT * h + HT), order[0]
+        return [
+            pltpu.make_async_copy(
+                stack.at[dates, g + j],
+                win.at[g, dates, :, 8 + 8 * j : 16 + 8 * j, :],
+                win_sem.at[G if h else g, j + 1],
+            )
+            for j in (-1, 0, 1)
+        ]
 
     order = [(i + 1) % G for i in range(G)]
     taps = [
@@ -84,10 +91,8 @@
     ]
     for cp in taps:
         cp.start()
-    early(0).start()
-    early(1).start()
-    for g in order[1:]:
-        window(g).start()
+    for cp in early(0) + early(1):
+        cp.start()
     metas = [
         pltpu.make_async_copy(ref, mloc.at[i], ml_sem.at[i])
         for i, ref in enumerate((ftile, frow, fcount, fowner))
@@ -128,12 +133,11 @@
         dates = slice(t0, t0 + nt)
 
         def row_pass(t, carry):
-            for p in range(ND):
-                cols = slice(p * CB, (p + 1) * CB)
-                acc = spat[0] * win[g, t, 2:10, cols]
+            for n in range(NL):
+                acc = spat[0] * win[g, t, n, 2:10, :]
                 for k in range(1, 2 * RAD + 1):
-                    acc = acc + spat[k] * win[g, t, 2 + k : 10 + k, cols]
-                rp[p + 1, t] = acc
+                    acc = acc + spat[k] * win[g, t, n, 2 + k : 10 + k, :]
+                rp[n // 2 + 1, t, :, (n % 2) * 128 : (n % 2) * 128 + 128] = acc
             return carry
 
         lax.fori_loop(t0, t0 + nt, row_pass, 0)
@@ -145,7 +149,9 @@
         low = low + dot(eh, b1h[...]) + dot(el, b1h[...]) + dot(eh, b1l[...])
         low = low.reshape(ND, nt, 8, CB)
         for p in range(ND):
-            sbuf[p, g, dates] = win[g, dates, 8:16, p * CB : (p + 1) * CB] - low[p]
+            for n in range(2):
+                lanes = slice(n * 128, n * 128 + 128)
+                sbuf[p, g, dates, :, lanes] = win[g, dates, 2 * p + n, 8:16, :] - low[p, :, :, lanes]
 
     def bulk(g, k, into=rbuf):
         p = (d + k) % ND
@@ -158,6 +164,17 @@
             device_id_type=MESH,
         )
 
+    def pair(g, k):
+        p = (d + k) % ND
+        return pltpu.make_async_remote_copy(
+            src_ref=sbuf.at[p, pl.ds(g, 2)],
+            dst_ref=rbuf.at[pl.ds(g, 2), pl.ds(TL * d, TL)],
+            send_sem=bulk_s.at[g, k],
+            recv_sem=bulk_r.at[g, k],
+            device_id=(p, s),
+            device_id_type=MESH,
+        )
+
     def half(h, k):
         g, p = order[0], (d + k) % ND
         return pltpu.make_async_remote_copy(
@@ -183,8 +200,8 @@
         )
 
     def halo(down):
-        src = stack.at[:, R - 8 : R, :] if down else stack.at[:, 0:8, :]
-        dst = win.at[0, :, 0:8, :] if down else win.at[G - 1, :, 16:24, :]
+        src = stack.at[:, G - 1] if down else stack.at[:, 0]
+        dst = win.at[0, :, :, 0:8, :] if down else win.at[G - 1, :, :, 16:24, :]
         i = 0 if down else 1
         to = (s + 1) % NS if down else (s + NS - 1) % NS
         return pltpu.make_async_remote_copy(
@@ -199,19 +216,27 @@
         )
 
     def wait_window(g):
-        pltpu.make_async_copy(stack.at[:, 0:24, :], win.at[g], win_sem.at[g]).wait()
-
-    early(0).wait()
+        for j in (-1, 0, 1):
+            pltpu.make_async_copy(
+                stack.at[:, g + j], win.at[g, :, :, 8 + 8 * j : 16 + 8 * j, :], win_sem.at[g, j + 1]
+            ).wait()
+
+    for cp in early(0):
+        cp.wait()
     filter_chunk(order[0], 0)
     pl.semaphore_wait(bar, jnp.where(d == 0, ND - 1 + NS - 1, ND - 1))
     send_half(0)
+    for g in order[1:]:
+        for cp in window(g):
+            cp.start()
 
     @pl.when(d == 0)
     def _():
         for k in range(1, NS):
             pl.semaphore_signal(group_in, inc=1, device_id=(0, (s + k) % NS), device_id_type=MESH)
 
-    early(1).wait()
+    for cp in early(1):
+        cp.wait()
     filter_chunk(order[0], HT)
     send_half(1)
     for cp in metas:
@@ -222,10 +247,16 @@
     def interior(g, carry):
         wait_window(g)
         filter_chunk(g)
-        send_chunk(g)
+        return carry
+
+    def two(i, carry):
+        lax.fori_loop(3 + 2 * i, 5 + 2 * i, interior, 0)
+        for k in range(1, ND):
+            pair(3 + 2 * i, k).start()
         return carry
 
     lax.fori_loop(2, 3, interior, 0)
+    send_chunk(2)
 
     @pl.when(d == 0)
     def _():
@@ -233,7 +264,7 @@
         for k in range(1, ND):
             pl.semaphore_signal(all_in, inc=1, device_id=(k, s), device_id_type=MESH)
 
-    lax.fori_loop(3, 4, interior, 0)
+    lax.fori_loop(0, 1, two, 0)
 
     @pl.when(d != 0)
     def _():
@@ -242,7 +273,7 @@
     halo(True).start()
     halo(False).start()
 
-    lax.fori_loop(4, G - 1, interior, 0)
+    lax.fori_loop(1, 2, two, 0)
 
     r_, c_ = iota((T, T), 0), iota((T, T), 1)
     r2, c2 = iota((T, 2 * T), 0), iota((T, 2 * T), 1) % T
@@ -266,15 +297,16 @@
     halo(True).wait()
     halo(False).wait()
     for g in (0, G - 1):
-        window(g).wait()
+        for cp in window(g):
+            cp.wait()
 
     @pl.when(s == 0)
     def _():
-        win[0, :, 0:8, :] = jnp.zeros((TL, 8, C), F32)
+        win[0, :, :, 0:8, :] = jnp.zeros((TL, NL, 8, 128), F32)
 
     @pl.when(s == NS - 1)
     def _():
-        win[G - 1, :, 16:24, :] = jnp.zeros((TL, 8, C), F32)
+        win[G - 1, :, :, 16:24, :] = jnp.zeros((TL, NL, 8, 128), F32)
 
     def edge_chunk(i, carry):
         filter_chunk((G - 1) * i)
@@ -342,23 +374,38 @@
     def result(g):
         return pltpu.make_async_copy(rbuf.at[g], gat_out.at[g], out_sem.at[g])
 
-    def finish(g, carry):
+    def complete(g):
+        filter_dates(rbuf.at[g], fbuf, rbuf.at[g], temp)
+        result(g).start()
+
+    def finish_single(i, carry):
+        g = 2 - 2 * i
         keep(g).wait()
         for k in range(1, ND):
             bulk(g, k).wait()
         complete(g)
         return carry
 
-    def complete(g):
-        filter_dates(rbuf.at[g], fbuf, rbuf.at[g], temp)
-        result(g).start()
+    def finish_two(i, carry):
+        g = 3 + 2 * i
+        for k in range(1, ND):
+            pair(g, k).wait()
+        for j in range(2):
+            keep(g + j).wait()
+        lax.fori_loop(g, g + 2, finish_one, 0)
+        return carry
+
+    def finish_one(g, carry):
+        complete(g)
+        return carry
 
     keep(order[0]).wait()
     for k in range(1, ND):
         half(0, k).wait()
         half(1, k).wait()
-    complete(order[0])
-    lax.fori_loop(2, G - 1, finish, 0)
+    lax.fori_loop(order[0], order[0] + 1, finish_one, 0)
+    lax.fori_loop(0, 1, finish_single, 0)
+    lax.fori_loop(0, 2, finish_two, 0)
 
     for k in range(1, ND):
         stage1(k).wait()
@@ -382,7 +429,7 @@
         stage2(k).start()
     z2[s] = y2[s]
 
-    lax.fori_loop(0, 1, finish, 0)
+    lax.fori_loop(1, 2, finish_single, 0)
 
     for k in range(1, NS):
         stage2(k).wait()
@@ -457,7 +504,7 @@
     vm, dma = pltpu.VMEM, pltpu.SemaphoreType.DMA
     sm = pltpu.SMEM
     scratch = [
-        sm((2 * RAD + 1,), F32), sm((2, 5), F32), vm((G, TL, 24, C), F32), vm((ND + 2, TL, 8, CB), F32),
+        sm((2 * RAD + 1,), F32), sm((2, 5), F32), vm((G, TL, NL, 24, 128), F32), vm((ND + 2, TL, 8, CB), F32),
         vm((CB, CB), BF16), vm((CB, CB), BF16), vm((CB, CB), BF16), vm((CB, CB), BF16),
         vm((ND, G, TL, 8, CB), F32), vm((G, T, 8, CB), F32), vm((T, 8, CB), F32),
         vm((4, 1, F), I32), vm((ND, 4, 1, F), I32),
@@ -465,7 +512,7 @@
         vm((ND, NS, F), F32), vm((8 * F, 8 * F), BF16), vm((8 * F, 8 * F), BF16),
         vm((NS, 1, 9 * F), F32), vm((NS, 1, 9 * F), F32), vm((NS, 9 * F), F32),
         vm((2 * F, F), F32), vm((T, 2 * F), F32), vm((1, F), F32),
-        dma((2,)), dma((G + 1,)), dma((4,)), dma((2,)), dma((2,)), dma((ND,)), dma((ND,)),
+        dma((2,)), dma((G + 1, 3)), dma((4,)), dma((2,)), dma((2,)), dma((ND,)), dma((ND,)),
         dma((G + 1, ND)), dma((G + 1, ND)), dma((ND,)), dma((ND,)), dma((NS,)), dma((NS,)),
         dma((G,)), dma((G,)), dma((2,)),
         pltpu.SemaphoreType.REGULAR, pltpu.SemaphoreType.REGULAR,
@@ -473,7 +520,7 @@
     held = [
         pltpu.with_memory_space_constraint(a, pltpu.HBM)
         for a in (
-            stack, spatial_taps, temporal_taps, foot_tile.reshape(1, F), foot_row.reshape(1, F),
+            stack.reshape(TL, G, 8, NL, 128).swapaxes(2, 3), spatial_taps, temporal_taps, foot_tile.reshape(1, F), foot_row.reshape(1, F),
             foot_count.reshape(1, F), foot_owner.reshape(1, F),
         )
     ]

time: 58.5 us -> 58.1 us (level)
  no operation moved by 1% of the time
where the time goes in v5:
time: 58.1 us; the launch traced here: 58 us
  Pallas kernels  57.3 us (99%)
  between operations  0.66 us (1%)
    pallas_call x1, Pallas kernels, shards(): pl.pallas_call(kernel, out_shape=(jax.ShapeDtypeStruct((G, T, 8, CB), F32...  55.2 us
    pallas_call x1, Pallas kernels, shards(): pl.pallas_call(finish_kernel, out_shape=(jax.ShapeDtypeStruct((T, R, CB),...  2.17 us

profile of v5, /device:TPU:1, one launch (start us, length us, event | category | flops | bytes accessed | tf_op | source)
XLA Modules:
  0.0 58.0 jit_solution(2434058984328760735)
XLA Ops:
  0.6 0.0 copy-start
  0.6 55.2 %series.1 = (f32[8,64,8,256]{3,2,1,0:T(8,128)S(1)}, f32[64,256]{1,0:T(8,128)S(1)}, f32[1,128]{1,0:T(1,128)S(1)}) custom-call(f32[8,8,16,8,128]{4,3,2,1,0:T(8,128)} %bitcast.11, f32[13]{0:T(128)} %spat_in.1, f32[2,5]{1,0:T(2,128)} %temp_in.3, s32[1,128]{1,0:T(1,128)} %bitcast.12, s32[1,128]{1,0:T(1,128)} %bitcast.13, s32[1,128]{1,0:T(1,128)} %bitcast.14, ...), custom_call_target="tpu_custom_call" | custom-call | tf_op jit(solution)/shard_map/series/pallas_call | solution.py:527
  55.8 0.0 copy-done
  55.8 2.2 %finish.1 = (f32[64,64,256]{2,1,0:T(8,128)}, f32[64,256]{1,0:T(8,128)}, f32[1,128]{1,0:T(1,128)}) custom-call(f32[8,64,8,256]{3,2,1,0:T(8,128)S(1)} %get-tuple-element.9.gat, f32[64,256]{1,0:T(8,128)S(1)} %get-tuple-element.10.anom, f32[1,128]{1,0:T(1,128)S(1)} %get-tuple-element.11.asset, f32[2,5]{1,0:T(2,128)S(1)} %copy-done), custom_call_target="tpu_custom_call" | custom-call | tf_op jit(solution)/shard_map/finish/pallas_call | solution.py:542
Async XLA Ops:
  0.6 55.2 %copy-start = (f32[2,5]{1,0:T(2,128)S(1)}, f32[2,5]{1,0:T(2,128)}, u32[]{:S(2)}) copy-start(f32[2,5]{1,0:T(2,128)} %temp_in.3) | copy-start | bytes 124

commit v6 on v5

--- a/solution.py
+++ b/solution.py
@@ -14,6 +14,7 @@
 C, CB, NL = 2048, 256, 16
 F = 128
 RAD = 6
+FAR_FIRST = (4, 5, 2, 6, 3, 7, 1)
 HT = 4
 
 
@@ -153,8 +154,11 @@
                 lanes = slice(n * 128, n * 128 + 128)
                 sbuf[p, g, dates, :, lanes] = win[g, dates, 2 * p + n, 8:16, :] - low[p, :, :, lanes]
 
+    def peer(k):
+        return (d // 2 + k // 2) % (ND // 2) * 2 + (d + k) % 2
+
     def bulk(g, k, into=rbuf):
-        p = (d + k) % ND
+        p = peer(k)
         return pltpu.make_async_remote_copy(
             src_ref=sbuf.at[p, g],
             dst_ref=into.at[g, pl.ds(TL * d, TL)],
@@ -165,7 +169,7 @@
         )
 
     def pair(g, k):
-        p = (d + k) % ND
+        p = peer(k)
         return pltpu.make_async_remote_copy(
             src_ref=sbuf.at[p, pl.ds(g, 2)],
             dst_ref=rbuf.at[pl.ds(g, 2), pl.ds(TL * d, TL)],
@@ -176,7 +180,7 @@
         )
 
     def half(h, k):
-        g, p = order[0], (d + k) % ND
+        g, p = order[0], peer(k)
         return pltpu.make_async_remote_copy(
             src_ref=sbuf.at[p, g, pl.ds(HT * h, HT)],
             dst_ref=rbuf.at[g, pl.ds(TL * d + HT * h, HT)],
@@ -187,11 +191,11 @@
         )
 
     def send_half(h):
-        for k in range(1, ND):
+        for k in FAR_FIRST:
             half(h, k).start()
 
     def send_chunk(g, into=rbuf):
-        for k in range(1, ND):
+        for k in FAR_FIRST:
             bulk(g, k, into).start()
 
     def keep(g, into=rbuf):
@@ -251,7 +255,7 @@
 
     def two(i, carry):
         lax.fori_loop(3 + 2 * i, 5 + 2 * i, interior, 0)
-        for k in range(1, ND):
+        for k in FAR_FIRST:
             pair(3 + 2 * i, k).start()
         return carry
 

time: 58.1 us -> 57.8 us (level)
  no operation moved by 1% of the time
where the time goes in v6:
time: 57.8 us; the launch traced here: 57.7 us
  Pallas kernels  57 us (99%)
  between operations  0.66 us (1%)
    pallas_call x1, Pallas kernels, shards(): pl.pallas_call(kernel, out_shape=(jax.ShapeDtypeStruct((G, T, 8, CB), F32...  54.9 us
    pallas_call x1, Pallas kernels, shards(): pl.pallas_call(finish_kernel, out_shape=(jax.ShapeDtypeStruct((T, R, CB),...  2.17 us

profile of v6, /device:TPU:1, one launch (start us, length us, event | category | flops | bytes accessed | tf_op | source)
XLA Modules:
  0.0 57.7 jit_solution(16516879729904192591)
XLA Ops:
  0.6 0.0 copy-start
  0.6 54.9 %series.1 = (f32[8,64,8,256]{3,2,1,0:T(8,128)S(1)}, f32[64,256]{1,0:T(8,128)S(1)}, f32[1,128]{1,0:T(1,128)S(1)}) custom-call(f32[8,8,16,8,128]{4,3,2,1,0:T(8,128)} %bitcast.11, f32[13]{0:T(128)} %spat_in.1, f32[2,5]{1,0:T(2,128)} %temp_in.3, s32[1,128]{1,0:T(1,128)} %bitcast.12, s32[1,128]{1,0:T(1,128)} %bitcast.13, s32[1,128]{1,0:T(1,128)} %bitcast.14, ...), custom_call_target="tpu_custom_call" | custom-call | tf_op jit(solution)/shard_map/series/pallas_call | solution.py:531
  55.5 0.0 copy-done
  55.5 2.2 %finish.1 = (f32[64,64,256]{2,1,0:T(8,128)}, f32[64,256]{1,0:T(8,128)}, f32[1,128]{1,0:T(1,128)}) custom-call(f32[8,64,8,256]{3,2,1,0:T(8,128)S(1)} %get-tuple-element.9.gat, f32[64,256]{1,0:T(8,128)S(1)} %get-tuple-element.10.anom, f32[1,128]{1,0:T(1,128)S(1)} %get-tuple-element.11.asset, f32[2,5]{1,0:T(2,128)S(1)} %copy-done), custom_call_target="tpu_custom_call" | custom-call | tf_op jit(solution)/shard_map/finish/pallas_call | solution.py:546
Async XLA Ops:
  0.6 54.9 %copy-start = (f32[2,5]{1,0:T(2,128)S(1)}, f32[2,5]{1,0:T(2,128)}, u32[]{:S(2)}) copy-start(f32[2,5]{1,0:T(2,128)} %temp_in.3) | copy-start | bytes 124
